TPU v7x, 512 devices: a whole 4x8x8 slice. The times are simulated.
512 devices in a mesh: band: 128 (over y, z, core), det: 4 (over x).
Axes of the slice: x: 4, y: 8, z: 8, core: 2. Of those that a mesh axis runs over, the one named last changes fastest.
Arguments:
- sky_coeffs: float32 [3, 2, 128, 2048], P(None, None, 'band', 'det'), may hold values from -6 to 6
- beam_coeffs: bfloat16 [4, 3, 2, 17, 2048], P('det'), may hold values from -2.5 to 2.5
- wigner_panel: bfloat16 [128, 17, 2048, 128], P('band', None, 'det'), may hold values from -0.125 to 0.125
- m_values: int32 [128], replicated, may hold values from 0 to 4095, as said below
- cycle_table: int32 [128, 3], replicated, may hold values from -1 to 127, as said below
- send_lists: int32 [4, 128, 128, 2], P('det'), may hold values from -1 to 12287, as said below
- sample_block: int32 [4, 524288], P('det', 'band'), may hold values from 0 to 255, as said below
- sample_phi: int32 [4, 524288], P('det', 'band'), may hold values from 0 to 126
- sample_psi: int32 [4, 524288], P('det', 'band'), may hold values from 0 to 31
- sample_frac: float32 [2, 4, 524288], P(None, 'det', 'band'), may hold values from 0 to 1
Outputs:
- timestream: float32 [4, 524288], P('det', 'band')
Inputs may be any that keep to these rules, and one draw needn't show every extreme that they name: `cycle_table`: each cycle stands in exactly one slot; -1 marks an empty slot; some cycle band fills all 3 slots, many hold none. `send_lists`: of one detector's entries from all bands to one owner, at most 8 are not -1, and every owner reaches 8; an entry from a band that holds no cycle is -1; an entry that is not -1 is slot * 4096 + start, with slot a filled slot of band src and start the block's first phi cell. `sample_block`: src * 2 + entry of an entry that is not -1 in the detector's list from band src to the sample's owner. `m_values`: distinct orders; 0 and 4095 among them.
All inputs are finite; a program needn't handle non-finite values.
Results may differ from a plain program's by a relative error of at most 0.0051.
Values may be sent and summed in bfloat16 or wider, within the bound.
A program may use at most 64 MiB of HBM per device.

v0:
```python
import math

import jax
import jax.numpy as jnp
from jax import lax
from jax.sharding import PartitionSpec as P

BMAX = 8
MPRIME = 17
NPSI = 32
NPHI = 4096
BLOCK_PHI = 128


def psi_tables():
    cells = jnp.arange(NPSI, dtype=jnp.int32)
    orders = jnp.arange(MPRIME, dtype=jnp.int32) - BMAX
    turns = orders[:, None] * cells[None, :] % NPSI
    angle = 2.0 * math.pi / NPSI * turns.astype(jnp.float32)
    return (jnp.cos(angle), jnp.sin(angle))


def psi_items(incoming):
    highest = lax.Precision.HIGHEST
    cos_psi, sin_psi = psi_tables()
    real_part = jnp.einsum(
        "bimn,nj->bimj", incoming[:, :, 0], cos_psi, precision=highest
    ) - jnp.einsum("bimn,nj->bimj", incoming[:, :, 1], sin_psi, precision=highest)
    imag_part = jnp.einsum(
        "bimn,nj->bimj", incoming[:, :, 0], sin_psi, precision=highest
    ) + jnp.einsum("bimn,nj->bimj", incoming[:, :, 1], cos_psi, precision=highest)
    return jnp.stack([real_part, imag_part], 2).astype(jnp.bfloat16)


def phi_table(m_values, columns):
    turns = m_values[:, None] * columns[None, :] % NPHI
    angle = 2.0 * math.pi / NPHI * turns.astype(jnp.float32)
    return jnp.concatenate([jnp.cos(angle), -jnp.sin(angle)], 0).astype(jnp.bfloat16)


def cycle_cube(samples, table, scale):
    bands, items, parts, local_orders, cells = samples.shape
    rows = jnp.transpose(samples, (1, 4, 2, 0, 3)).reshape(
        items * cells, parts * bands * local_orders
    )
    values = jnp.dot(rows, table, preferred_element_type=jnp.float32) * scale
    return values.astype(jnp.bfloat16).reshape(items, cells, table.shape[1])


def interpolate(flat_cells, block_pos, cell_phi, cell_psi, frac_phi, frac_psi):
    psi_next = (cell_psi + 1) % NPSI
    base_index = block_pos * (NPSI * BLOCK_PHI)
    low_index = base_index + cell_psi * BLOCK_PHI + cell_phi
    high_index = base_index + psi_next * BLOCK_PHI + cell_phi
    value_ll = jnp.take(flat_cells, low_index).astype(jnp.float32)
    value_lh = jnp.take(flat_cells, low_index + 1).astype(jnp.float32)
    value_hl = jnp.take(flat_cells, high_index).astype(jnp.float32)
    value_hh = jnp.take(flat_cells, high_index + 1).astype(jnp.float32)
    low_row = (1.0 - frac_phi) * value_ll + frac_phi * value_lh
    high_row = (1.0 - frac_phi) * value_hl + frac_phi * value_hh
    return (1.0 - frac_psi) * low_row + frac_psi * high_row


def per_device(
    sky_coeffs,
    beam_coeffs,
    wigner_panel,
    m_values,
    cycle_table,
    send_lists,
    sample_block,
    sample_phi,
    sample_psi,
    sample_frac,
):
    highest = lax.Precision.HIGHEST
    orders_all = m_values.shape[0]
    scale = 2.0 / math.sqrt(orders_all * MPRIME)
    own_band = lax.axis_index("band")
    beams = lax.all_to_all(beam_coeffs, "det", split_axis=4, concat_axis=0, tiled=True).astype(
        jnp.float32
    )
    mix_real = jnp.einsum(
        "cmk,dcnk->dmnk", sky_coeffs[:, 0], beams[:, :, 0], precision=highest
    ) + jnp.einsum("cmk,dcnk->dmnk", sky_coeffs[:, 1], beams[:, :, 1], precision=highest)
    mix_imag = jnp.einsum(
        "cmk,dcnk->dmnk", sky_coeffs[:, 1], beams[:, :, 0], precision=highest
    ) - jnp.einsum("cmk,dcnk->dmnk", sky_coeffs[:, 0], beams[:, :, 1], precision=highest)
    mixed = jnp.stack([mix_real, mix_imag], 1).astype(jnp.bfloat16)
    coeff = lax.psum_scatter(
        jnp.einsum("dsmnk,mnkr->dsmnr", mixed, wigner_panel, preferred_element_type=jnp.float32),
        "det",
        scatter_dimension=0,
        tiled=True,
    )[0]
    lists = send_lists[0]
    cycle_index = jnp.maximum(cycle_table, 0)
    table = phi_table(m_values, jnp.arange(NPHI, dtype=jnp.int32))
    payload = jnp.transpose(jnp.take(coeff, cycle_index, axis=3), (3, 4, 0, 1, 2))
    cube = cycle_cube(
        psi_items(lax.all_to_all(payload, "band", split_axis=0, concat_axis=0, tiled=True)),
        table,
        scale,
    )
    my_codes = jnp.maximum(lax.dynamic_index_in_dim(lists, own_band, 0, keepdims=False), 0)
    slot_index = my_codes // NPHI
    start_cell = my_codes % NPHI
    wrapped = jnp.concatenate([cube, cube[:, :, :BLOCK_PHI]], 2)

    def cut_block(slot_one, start_one):
        return lax.dynamic_slice(wrapped, (slot_one, 0, start_one), (1, NPSI, BLOCK_PHI))[0]

    outgoing = jax.vmap(jax.vmap(cut_block))(slot_index, start_cell)
    received = lax.all_to_all(outgoing, "band", split_axis=0, concat_axis=0, tiled=True)
    flat_cells = received.reshape(-1)
    block_pos = sample_block[0]
    values = interpolate(
        flat_cells, block_pos, sample_phi[0], sample_psi[0], sample_frac[0, 0], sample_frac[1, 0]
    )
    return values[None, :]


def solution(mesh):
    return jax.shard_map(
        per_device,
        mesh=mesh,
        in_specs=(
            P(None, None, "band", "det"),
            P("det", None, None, None, None),
            P("band", None, "det", None),
            P(),
            P(),
            P("det", None, None, None),
            P("det", "band"),
            P("det", "band"),
            P("det", "band"),
            P(None, "det", "band"),
        ),
        out_specs=P("det", "band"),
        check_vma=False,
    )
```

profile of v0, /device:TPU:26, one launch (start us, length us, event | category | flops | bytes accessed | tf_op | source)
XLA Modules:
  0.0 492.7 jit_solution(9757303556894049428)
XLA Ops:
  6.5 8.0 %copy.48 = bf16[1,3,2,17,2048]{3,2,1,0,4:T(2,128)(2,1)} copy(bf16[1,3,2,17,2048]{4,2,3,1,0:T(2,128)(2,1)} %param.13) | data formatting | bytes 835584 | tf_op args[1]
  14.6 6.3 %reshape.301 = bf16[4,2,26112]{2,1,0:T(2,128)(2,1)} reshape(bf16[2048,1,3,2,17]{4,3,2,1,0:T(2,128)(2,1)} %bitcast.146) | data formatting | bytes 835584
  20.9 4.8 all-to-all-start
  26.2 9.7 %cosine_convert_fusion = (bf16[128,4096]{1,0:T(8,128)(2,1)}, bf16[128,4096]{1,0:T(8,128)(2,1)}) fusion(s32[128]{0:T(128)S(1)} %copy-done.7), kind=kLoop, calls=%fused_computation.20 | loop fusion | flops 8912896 | bytes 2097664 | tf_op jit(solution)/shard_map/convert
  36.0 0.7 fusion.63
  36.9 1.3 dynamic-slice.1
  38.2 7.9 %reshape.302 = bf16[2048,1,3,2,17]{4,3,2,1,0:T(2,128)(2,1)} reshape(bf16[4,2,26112]{2,1,0:T(2,128)(2,1)S(1)} %all-to-all-done) | data formatting | bytes 835584
  46.1 7.4 %copy.49 = bf16[1,3,2,17,4,512]{5,4,3,1,2,0:T(4,128)(2,1)S(1)} copy(bf16[1,3,2,17,4,512]{3,2,1,5,4,0:T(2,128)(2,1)} %bitcast.145) | data formatting | bytes 835584 | tf_op jit(solution)/shard_map/all_to_all | solution.py:80
  53.5 0.5 fusion.21
  54.1 0.5 fusion.12
  54.6 0.7 copy.50
  55.3 55.2 %all-reduce.3.cloned.1.call-done = f32[4,2,1,17,128]{4,1,3,2,0:T(2,128)} async-done(((f32[4,2,1,17,128]{4,1,3,2,0:T(2,128)}), f32[4,2,1,17,128]{4,1,3,2,0:T(2,128)}) %all-reduce.3.cloned.1.call-update) | async-done | bytes 69648
  110.5 1.4 constant_dynamic-slice_fusion
  112.0 2.0 gather_fusion
  114.0 1.2 select_bitcast_fusion
  115.3 14.3 %all-to-all-start.1 = ((f32[128,3,2,1,17]{4,2,3,1,0:T(2,128)}), f32[128,3,2,1,17]{4,2,3,1,0:T(2,128)S(1)}, u32[]{:S(2)}, u32[]{:S(2)}) async-start(f32[128,3,2,1,17]{4,2,3,1,0:T(2,128)} %select_bitcast_fusion), calls=%async_computation.1 | async-start | bytes 786432 | tf_op jit(solution)/shard_map/all_to_all | solution.py:101
  129.6 15.7 %all-to-all-done.1 = f32[128,3,2,1,17]{4,2,3,1,0:T(2,128)S(1)} async-done(((f32[128,3,2,1,17]{4,2,3,1,0:T(2,128)}), f32[128,3,2,1,17]{4,2,3,1,0:T(2,128)S(1)}, u32[]{:S(2)}, u32[]{:S(2)}) %all-to-all-start.1) | async-done | bytes 52256 | tf_op jit(solution)/shard_map/all_to_all | solution.py:101
  145.8 0.4 fusion.34
  146.2 0.4 fusion.32
  146.7 0.4 fusion.18
  147.1 0.4 fusion.17
  147.5 2.0 fusion
  149.6 4.7 copy.58
  154.3 40.9 %gather_fusion.1 = bf16[256,32,128]{1,0,2:T(8,128)(2,1)} fusion(bf16[3,32,4224]{1,0,2:T(4,128)(2,1)} %copy.58, s32[256]{0:T(256)S(1)} %reshape.266), kind=kCustom, calls=%fused_computation.5 | custom fusion | bytes 4197376 | tf_op jit(solution)/shard_map/vmap(vmap())/gather | solution.py:111
  195.2 17.0 %copy.59 = bf16[128,2,32,128]{3,2,1,0:T(8,128)(2,1)} copy(bf16[128,2,32,128]{2,1,0,3:T(2,128)(2,1)} %bitcast.144) | data formatting | bytes 4194304 | tf_op jit(solution)/shard_map/vmap(vmap())/squeeze | solution.py:111
  212.3 9.6 %all-to-all-start.2 = ((bf16[128,2,32,128]{3,2,1,0:T(8,128)(2,1)}), bf16[128,2,32,128]{3,2,1,0:T(8,128)(2,1)}, u32[]{:S(2)}, u32[]{:S(2)}) async-start(bf16[128,2,32,128]{3,2,1,0:T(8,128)(2,1)} %copy.59), calls=%async_computation.2 | async-start | bytes 4194304 | tf_op jit(solution)/shard_map/all_to_all | solution.py:114
  222.1 49.9 %all-to-all-done.2 = bf16[128,2,32,128]{3,2,1,0:T(8,128)(2,1)} async-done(((bf16[128,2,32,128]{3,2,1,0:T(8,128)(2,1)}), bf16[128,2,32,128]{3,2,1,0:T(8,128)(2,1)}, u32[]{:S(2)}, u32[]{:S(2)}) %all-to-all-start.2) | async-done | bytes 2097184 | tf_op jit(solution)/shard_map/all_to_all | solution.py:114
  272.0 53.6 %gather_fusion.4 = bf16[4096]{0:T(1024)(128)(2,1)S(1)} fusion(bf16[1048576]{0:T(1024)(128)(2,1)} %bitcast.51, s32[4096]{0:T(1024)S(1)} %get-tuple-element.31), kind=kCustom, calls=%fused_computation.2.clone | custom fusion | bytes 32768 | tf_op jit(solution)/shard_map/jit(_take)/gather | solution.py:57
  325.6 53.0 %gather_fusion.2 = bf16[4096]{0:T(1024)(128)(2,1)S(1)} fusion(bf16[1048576]{0:T(1024)(128)(2,1)} %bitcast.51, s32[4096]{0:T(1024)S(1)} %get-tuple-element.30), kind=kCustom, calls=%fused_computation.clone | custom fusion | bytes 32768 | tf_op jit(solution)/shard_map/jit(_take)/gather | solution.py:55
  378.6 53.0 %gather_fusion.3 = bf16[4096]{0:T(1024)(128)(2,1)S(1)} fusion(bf16[1048576]{0:T(1024)(128)(2,1)} %bitcast.51, s32[4096]{0:T(1024)S(1)} %get-tuple-element.18), kind=kCustom, calls=%fused_computation.1.clone | custom fusion | bytes 32768 | tf_op jit(solution)/shard_map/jit(_take)/gather | solution.py:56
  431.6 53.6 %gather_fusion.5 = bf16[4096]{0:T(1024)(128)(2,1)S(1)} fusion(bf16[1048576]{0:T(1024)(128)(2,1)} %bitcast.51, s32[4096]{0:T(1024)S(1)} %get-tuple-element.12), kind=kCustom, calls=%fused_computation.3.clone | custom fusion | bytes 32768 | tf_op jit(solution)/shard_map/jit(_take)/gather | solution.py:58
  485.2 0.6 multiply_add_fusion
  (45 shorter events, 1.8 us)
Async XLA Ops:
  6.5 47.6 %copy-start = (bf16[1,17,512,128]{3,2,1,0:T(8,128)(2,1)S(1)}, bf16[1,17,512,128]{3,2,1,0:T(8,128)(2,1)}, u32[]{:S(2)}) copy-start(bf16[1,17,512,128]{3,2,1,0:T(8,128)(2,1)} %param.14) | copy-start | bytes 6684676
  14.5 11.2 %copy-start.6 = (s32[128,3]{0,1:T(4,128)S(1)}, s32[128,3]{0,1:T(4,128)}, u32[]{:S(2)}) copy-start(s32[128,3]{0,1:T(4,128)} %param.16) | copy-start | bytes 4612
  14.5 11.2 %copy-start.5 = (f32[3,2,1,512]{3,2,1,0:T(1,128)S(1)}, f32[3,2,1,512]{3,2,1,0:T(1,128)}, u32[]{:S(2)}) copy-start(f32[3,2,1,512]{3,2,1,0:T(1,128)} %param.12) | copy-start | bytes 36868
  14.5 11.7 %copy-start.7 = (s32[128]{0:T(128)S(1)}, s32[128]{0:T(128)}, u32[]{:S(2)}) copy-start(s32[128]{0:T(128)} %param.15) | copy-start | bytes 1540
  20.9 17.3 %all-to-all-start = ((bf16[4,2,26112]{2,1,0:T(2,128)(2,1)}), bf16[4,2,26112]{2,1,0:T(2,128)(2,1)S(1)}, u32[]{:S(2)}, u32[]{:S(2)}) async-start(bf16[4,2,26112]{2,1,0:T(2,128)(2,1)} %reshape.301), calls=%async_computation | async-start | bytes 835584 | tf_op jit(solution)/shard_map/all_to_all | solution.py:80
  25.7 84.8 %all-reduce.3.cloned.1.call-start = ((), (), s32[]{:S(2)}) async-start(), calls=%async_computation.3 | async-start | bytes 139264
  115.3 30.1 %all-to-all-start.1 = ((f32[128,3,2,1,17]{4,2,3,1,0:T(2,128)}), f32[128,3,2,1,17]{4,2,3,1,0:T(2,128)S(1)}, u32[]{:S(2)}, u32[]{:S(2)}) async-start(f32[128,3,2,1,17]{4,2,3,1,0:T(2,128)} %select_bitcast_fusion), calls=%async_computation.1 | async-start | bytes 786432 | tf_op jit(solution)/shard_map/all_to_all | solution.py:101
  212.3 9.7 %copy-start.3 = (s32[1,4096]{1,0:T(1,128)S(1)}, s32[1,4096]{1,0:T(1,128)}, u32[]{:S(2)}) copy-start(s32[1,4096]{1,0:T(1,128)} %param.18) | copy-start | bytes 49156
  212.3 9.7 %copy-start.2 = (s32[1,4096]{1,0:T(1,128)S(1)}, s32[1,4096]{1,0:T(1,128)}, u32[]{:S(2)}) copy-start(s32[1,4096]{1,0:T(1,128)} %param.20) | copy-start | bytes 49156
  212.3 9.7 %copy-start.4 = (s32[1,4096]{1,0:T(1,128)S(1)}, s32[1,4096]{1,0:T(1,128)}, u32[]{:S(2)}) copy-start(s32[1,4096]{1,0:T(1,128)} %param.19) | copy-start | bytes 49156
  212.3 9.8 %copy-start.1 = (f32[2,1,4096]{2,1,0:T(1,128)S(1)}, f32[2,1,4096]{2,1,0:T(1,128)}, u32[]{:S(2)}) copy-start(f32[2,1,4096]{2,1,0:T(1,128)} %param.21) | copy-start | bytes 98308
  212.3 59.7 %all-to-all-start.2 = ((bf16[128,2,32,128]{3,2,1,0:T(8,128)(2,1)}), bf16[128,2,32,128]{3,2,1,0:T(8,128)(2,1)}, u32[]{:S(2)}, u32[]{:S(2)}) async-start(bf16[128,2,32,128]{3,2,1,0:T(8,128)(2,1)} %copy.59), calls=%async_computation.2 | async-start | bytes 4194304 | tf_op jit(solution)/shard_map/all_to_all | solution.py:114
Sparse Core Ops, SparseCore 0:
  55.4 55.0 all-reduce.2
where the time goes:
time: 500 us; the launch traced here: 493 us
  local copies, waits for them, and re-layouts  312 us (62%)
  waiting for transfers between devices  121 us (24%)
  starting transfers between devices  28.8 us (6%)
  between operations  13.7 us (3%)
  other arithmetic  13.1 us (3%)
    unnamed x2, waiting for transfers between devices  55.2 us
    gather x1, local copies, waits for them, and re-layouts, interpolate(): value_hh = jnp.take(flat_cells, high_index + 1).astype(jnp.float32)  53.6 us
    gather x1, local copies, waits for them, and re-layouts, interpolate(): value_hl = jnp.take(flat_cells, high_index).astype(jnp.float32)  53.6 us
    gather x1, local copies, waits for them, and re-layouts, interpolate(): value_ll = jnp.take(flat_cells, low_index).astype(jnp.float32)  53 us
    gather x1, local copies, waits for them, and re-layouts, interpolate(): value_lh = jnp.take(flat_cells, low_index + 1).astype(jnp.float32)  53 us
    all_to_all x1, waiting for transfers between devices, per_device(): lax.all_to_all(outgoing, 'band', split_axis=0, concat_axis=0, tiled=True)  49.9 us
    gather x1, local copies, waits for them, and re-layouts, cut_block(): lax.dynamic_slice(wrapped, (slot_one, 0, start_one), (1, NPSI, BLOCK_PHI))  40.9 us
    unnamed x24, local copies, waits for them, and re-layouts  25.1 us
  transfers between devices with their start and end apart: 4, of which 3 were waited for; matrix products, arithmetic and copies ran while one was open for 3% of the time, Pallas kernels for 0%

commit v1 on v0

v1 whole, which is shorter than its diff:
```python
import functools
import math

import jax
import jax.numpy as jnp
import numpy as np
from jax import lax
from jax.experimental import pallas as pl
from jax.experimental.pallas import tpu as pltpu
from jax.sharding import PartitionSpec as P

BMAX = 8
MPRIME = 17
NPSI = 32
NPHI = 4096
BLOCK_PHI = 128
BANDS = 128
LISTED = 8
ROWS = 4
ORDERS_PAD = 24
CHUNK = 512
UNLISTED = 200.0
MESH = pl.DeviceIdType.MESH


def psi_matrices():
    orders = np.arange(MPRIME) - BMAX
    cells = np.arange(128) % NPSI
    angle = 2.0 * math.pi / NPSI * ((orders[:, None] * cells[None, :]) % NPSI)
    cos_psi, sin_psi = np.cos(angle), np.sin(angle)
    table = np.zeros((2, 2, ORDERS_PAD, 128), np.float32)
    table[0, 0, :MPRIME] = cos_psi
    table[0, 1, :MPRIME] = -sin_psi
    table[1, 0, :MPRIME] = sin_psi
    table[1, 1, :MPRIME] = cos_psi
    return table


def cosine_weights():
    nodes = np.cos(math.pi * (np.arange(64) + 0.5) / 64)
    top = math.pi**2
    squares = (nodes + 1.0) * top / 2
    fit = np.polynomial.chebyshev.Chebyshev.fit(squares, np.cos(np.sqrt(squares)), 8, domain=[0, top])
    weights = fit.convert(kind=np.polynomial.Polynomial).coef
    return [float(w) for w in weights]


COSINE = cosine_weights()


def cosine_of_turns(turns):
    centred = jnp.bitwise_and(turns, NPHI - 1) - NPHI // 2
    angle = centred.astype(jnp.float32) * (2.0 * math.pi / NPHI)
    square = angle * angle
    total = jnp.full_like(square, COSINE[-1])
    for weight in COSINE[-2::-1]:
        total = total * square + weight
    return -total


def iota(shape, axis):
    return lax.broadcasted_iota(jnp.int32, shape, axis)


def dot(a, b):
    return jnp.dot(a, b, preferred_element_type=jnp.float32)


def dot_rows(a, b, precision=None):
    return lax.dot_general(
        a, b, (((0,), (0,)), ((), ())), preferred_element_type=jnp.float32, precision=precision
    )


def ones_where(mask):
    return jnp.where(mask, 1.0, 0.0).astype(jnp.bfloat16)


def list_ranks(codes):
    entries = codes.shape[0]
    listed = codes >= 0
    below = ones_where(iota((entries, entries), 0) > iota((entries, entries), 1))
    rank = dot(below, ones_where(listed))
    return jnp.where(listed, rank, UNLISTED)


def choose_payload(coeff, psi_table, codes, cycles):
    highest = lax.Precision.HIGHEST
    rank = list_ranks(codes)
    both = jnp.concatenate([cycles, cycles], 0)
    slot = lax.shift_right_arithmetic(codes, 12)
    cycle = jnp.where(slot == 0, both[:, 0:1], jnp.where(slot == 1, both[:, 1:2], both[:, 2:3]))
    width = BANDS * ROWS
    spread = ones_where(iota((BANDS, width), 1) // ROWS == iota((BANDS, width), 0))
    rank_wide = dot(rank.astype(jnp.bfloat16), spread)
    cycle_wide = dot(cycle.astype(jnp.float32).astype(jnp.bfloat16), spread)
    place = iota((1, width), 1) % ROWS
    half = place % 2
    lane_group = iota((BANDS, 128), 1) // NPSI
    waves = [
        dot_rows(coeff[0], psi_table[part, 0], highest)
        + dot_rows(coeff[1], psi_table[part, 1], highest)
        for part in range(2)
    ]
    row_cycle = iota((128, width), 0).astype(jnp.float32)
    total = None
    for group in range(4):
        wanted = (4 * half + group).astype(jnp.float32)
        chosen = jnp.sum(jnp.where(rank_wide == wanted, cycle_wide, 0.0), 0, keepdims=True)
        for part in range(2):
            target = jnp.where(place // 2 == part, chosen, -1.0)
            hot = ones_where(row_cycle == target)
            piece = jnp.where(lane_group == group, waves[part], 0.0).astype(jnp.bfloat16)
            term = dot_rows(hot, piece)
            total = term if total is None else total + term
    return total.astype(jnp.bfloat16)


def own_blocks(codes, owner):
    rank = list_ranks(codes)
    entries = codes.shape[0]
    mine = iota((entries, BANDS), 1) == owner
    rank_col = jnp.sum(jnp.where(mine, rank, 0.0), 1, keepdims=True)
    start = jnp.bitwise_and(codes, NPHI - 1).astype(jnp.float32)
    start_col = jnp.sum(jnp.where(mine, start, 0.0), 1, keepdims=True)
    place = iota((entries, 128), 0)
    name = (place % BANDS * 2 + place // BANDS + 1).astype(jnp.float32)
    lanes = iota((entries, 128), 1).astype(jnp.float32)
    picked = rank_col == lanes
    name_row = jnp.sum(jnp.where(picked, name, 0.0), 0, keepdims=True) - 1.0
    start_row = jnp.sum(jnp.where(picked, start_col, 0.0), 0, keepdims=True)
    rows = LISTED * NPSI
    of_row = iota((rows, 128), 0) // NPSI == iota((rows, 128), 1)
    name_col = jnp.sum(jnp.where(of_row, name_row, 0.0), 1, keepdims=True).astype(jnp.int32)
    keys = name_col * NPSI + iota((rows, 1), 0) % NPSI
    rows = LISTED * BLOCK_PHI
    of_row = iota((rows, 128), 0) // BLOCK_PHI == iota((rows, 128), 1)
    first = jnp.sum(jnp.where(of_row, start_row, 0.0), 1, keepdims=True).astype(jnp.int32)
    columns = first + iota((rows, 1), 0) % BLOCK_PHI
    return keys, columns


def block_cells(received, cos_phase, sin_phase, scale):
    width = BANDS * ROWS
    lane_group = iota((BANDS, 128), 1) // NPSI
    halves = []
    for half in range(2):
        total = None
        for part, phase in enumerate((cos_phase, sin_phase)):
            pick = ones_where(
                iota((BANDS, width), 1) == iota((BANDS, width), 0) * ROWS + (2 * part + half)
            )
            rows = dot(pick, received)
            for group in range(4):
                first = (4 * half + group) * BLOCK_PHI
                piece = jnp.where(lane_group == group, rows, 0.0).astype(jnp.bfloat16)
                term = dot(phase[first : first + BLOCK_PHI], piece)
                total = term if total is None else total + term
        halves.append((total * scale).astype(jnp.bfloat16))
    return jnp.concatenate(halves, 1)


def blend(cells, keys, block, cell_phi, cell_psi, frac_phi, frac_psi):
    count = block.shape[1]
    base = block * NPSI
    low = ones_where(keys == base + cell_psi)
    high = ones_where(keys == base + jnp.bitwise_and(cell_psi + 1, NPSI - 1))
    row = (1.0 - frac_psi) * dot(cells, low) + frac_psi * dot(cells, high)
    places = iota((BLOCK_PHI, count), 0)
    weight = jnp.where(places == cell_phi, 1.0 - frac_phi, 0.0)
    weight = jnp.where(places == cell_phi + 1, frac_phi, weight)
    return jnp.sum(weight * row, 0, keepdims=True)


def payload_kernel(coeff_ref, psi_ref, codes_ref, cycles_ref, out_ref):
    out_ref[...] = choose_payload(coeff_ref, psi_ref, codes_ref[...], cycles_ref[...])


def exchange_kernel(bands, src_ref, dst_ref, send_sem, recv_sem, own_sem):
    me = lax.axis_index("band")
    barrier = pltpu.get_barrier_semaphore()

    def greet(step, carry):
        peer = lax.rem(me + step, bands)
        pl.semaphore_signal(barrier, inc=1, device_id={"band": peer}, device_id_type=MESH)
        return carry

    lax.fori_loop(1, bands, greet, 0)
    own = pltpu.make_async_copy(src_ref.at[me], dst_ref.at[me], own_sem)
    own.start()
    pl.semaphore_wait(barrier, bands - 1)

    def send(step, carry):
        peer = lax.rem(me + step, bands)
        pltpu.make_async_remote_copy(
            src_ref=src_ref.at[peer],
            dst_ref=dst_ref.at[me],
            send_sem=send_sem,
            recv_sem=recv_sem,
            device_id={"band": peer},
            device_id_type=MESH,
        ).start()
        return carry

    lax.fori_loop(1, bands, send, 0)
    own.wait()
    others = pl.ds(0, bands - 1)
    everything = pltpu.make_async_remote_copy(
        src_ref=src_ref.at[others],
        dst_ref=dst_ref.at[others],
        send_sem=send_sem,
        recv_sem=recv_sem,
        device_id={"band": me},
        device_id_type=MESH,
    )
    everything.wait_send()
    everything.wait_recv()


def samples_kernel(
    scale,
    owner_ref,
    received_ref,
    codes_ref,
    orders_ref,
    block_ref,
    phi_ref,
    psi_ref,
    frac_ref,
    out_ref,
):
    keys, columns = own_blocks(codes_ref[...], owner_ref[0])
    turns = columns * orders_ref[...]
    cos_phase = cosine_of_turns(turns).astype(jnp.bfloat16)
    sin_phase = cosine_of_turns(turns + NPHI // 4).astype(jnp.bfloat16)
    cells = block_cells(received_ref[...], cos_phase, sin_phase, scale)
    for first in range(0, block_ref.shape[1], CHUNK):
        part = slice(first, first + CHUNK)
        out_ref[:, part] = blend(
            cells,
            keys,
            block_ref[:, part],
            phi_ref[:, part],
            psi_ref[:, part],
            frac_ref[0:1, part],
            frac_ref[1:2, part],
        )


def vmem_specs(count):
    return [pl.BlockSpec(memory_space=pltpu.VMEM)] * count


def per_device(
    sky_coeffs,
    beam_coeffs,
    wigner_panel,
    m_values,
    cycle_table,
    send_lists,
    sample_block,
    sample_phi,
    sample_psi,
    sample_frac,
):
    highest = lax.Precision.HIGHEST
    orders_all = m_values.shape[0]
    scale = 2.0 / math.sqrt(orders_all * MPRIME)
    own_band = lax.axis_index("band")
    beams = lax.all_to_all(beam_coeffs, "det", split_axis=4, concat_axis=0, tiled=True).astype(
        jnp.float32
    )
    mix_real = jnp.einsum(
        "cmk,dcnk->dmnk", sky_coeffs[:, 0], beams[:, :, 0], precision=highest
    ) + jnp.einsum("cmk,dcnk->dmnk", sky_coeffs[:, 1], beams[:, :, 1], precision=highest)
    mix_imag = jnp.einsum(
        "cmk,dcnk->dmnk", sky_coeffs[:, 1], beams[:, :, 0], precision=highest
    ) - jnp.einsum("cmk,dcnk->dmnk", sky_coeffs[:, 0], beams[:, :, 1], precision=highest)
    mixed = jnp.stack([mix_real, mix_imag], 1).astype(jnp.bfloat16)
    coeff = lax.psum_scatter(
        jnp.einsum("dsmnk,mnkr->dsmnr", mixed, wigner_panel, preferred_element_type=jnp.float32),
        "det",
        scatter_dimension=0,
        tiled=True,
    )[0]
    coeff = jnp.pad(coeff[:, 0], ((0, 0), (0, ORDERS_PAD - MPRIME), (0, 0)))
    codes = jnp.transpose(send_lists[0], (2, 0, 1)).reshape(2 * BANDS, BANDS)
    payload = pl.pallas_call(
        payload_kernel,
        out_shape=jax.ShapeDtypeStruct((BANDS * ROWS, 128), jnp.bfloat16),
        in_specs=vmem_specs(4),
        out_specs=vmem_specs(1)[0],
    )(coeff, jnp.asarray(psi_matrices()), codes, cycle_table)
    received = pl.pallas_call(
        functools.partial(exchange_kernel, BANDS),
        out_shape=jax.ShapeDtypeStruct((BANDS, ROWS, 128), jnp.bfloat16),
        in_specs=vmem_specs(1),
        out_specs=vmem_specs(1)[0],
        scratch_shapes=[pltpu.SemaphoreType.DMA] * 3,
        compiler_params=pltpu.CompilerParams(collective_id=0, has_side_effects=True),
    )(payload.reshape(BANDS, ROWS, 128))
    return pl.pallas_call(
        functools.partial(samples_kernel, scale),
        out_shape=jax.ShapeDtypeStruct(sample_block.shape, jnp.float32),
        in_specs=[pl.BlockSpec(memory_space=pltpu.SMEM)] + vmem_specs(7),
        out_specs=vmem_specs(1)[0],
    )(
        own_band.reshape(1),
        received.reshape(BANDS * ROWS, 128),
        codes,
        m_values.reshape(1, orders_all),
        sample_block,
        sample_phi,
        sample_psi,
        sample_frac[:, 0],
    )


def solution(mesh):
    return jax.shard_map(
        per_device,
        mesh=mesh,
        in_specs=(
            P(None, None, "band", "det"),
            P("det", None, None, None, None),
            P("band", None, "det", None),
            P(),
            P(),
            P("det", None, None, None),
            P("det", "band"),
            P("det", "band"),
            P("det", "band"),
            P(None, "det", "band"),
        ),
        out_specs=P("det", "band"),
        check_vma=False,
    )
```

time: 500 us -> 116 us (0.23)
  the two profiles are of different devices: /device:TPU:26 before, /device:TPU:1 now
where the time goes in v1:
time: 116 us; the launch traced here: 115 us
  local copies, waits for them, and re-layouts  33.6 us (29%)
  waiting for transfers between devices  33.2 us (29%)
  Pallas kernels  29 us (25%)
  between operations  13.5 us (12%)
  starting transfers between devices  4.83 us (4%)
    reduce_scatter x1, waiting for transfers between devices, per_device(): lax.psum_scatter(jnp.einsum('dsmnk,mnkr->dsmnr', mixed, wigner_panel, pre...  26.8 us
    unnamed x16, local copies, waits for them, and re-layouts  23.5 us
    pallas_call x1, Pallas kernels, per_device(): pl.pallas_call(functools.partial(exchange_kernel, BANDS), out_shape=jax.S...  21.7 us
    all_to_all x1, local copies, waits for them, and re-layouts, per_device(): lax.all_to_all(beam_coeffs, 'det', split_axis=4, concat_axis=0, tiled=True)  7.39 us
    all_to_all x1, waiting for transfers between devices, per_device(): lax.all_to_all(beam_coeffs, 'det', split_axis=4, concat_axis=0, tiled=True)  6.34 us
    all_to_all x1, starting transfers between devices, per_device(): lax.all_to_all(beam_coeffs, 'det', split_axis=4, concat_axis=0, tiled=True)  4.83 us
    pallas_call x1, Pallas kernels, per_device(): pl.pallas_call(functools.partial(samples_kernel, scale), out_shape=jax.Sh...  4.42 us
    pallas_call x1, Pallas kernels, per_device(): pl.pallas_call(payload_kernel, out_shape=jax.ShapeDtypeStruct((BANDS * RO...  2.91 us
  transfers between devices with their start and end apart: 2, of which 2 were waited for; matrix products, arithmetic and copies ran while one was open for 2% of the time, Pallas kernels for 0%

profile of v1, /device:TPU:1, one launch (start us, length us, event | category | flops | bytes accessed | tf_op | source)
XLA Modules:
  0.0 115.1 jit_solution(13244044238724071260)
XLA Ops:
  6.5 0.0 copy-start
  6.5 7.9 %copy.24 = bf16[1,3,2,17,2048]{3,2,1,0,4:T(2,128)(2,1)} copy(bf16[1,3,2,17,2048]{4,2,3,1,0:T(2,128)(2,1)} %param.12) | data formatting | bytes 835584 | tf_op args[1]
  14.5 0.0 copy-start.3
  14.5 6.3 %reshape.70 = bf16[4,2,26112]{2,1,0:T(2,128)(2,1)} reshape(bf16[2048,1,3,2,17]{4,3,2,1,0:T(2,128)(2,1)} %bitcast.72) | data formatting | bytes 835584
  20.8 4.8 %all-to-all-start = ((bf16[4,2,26112]{2,1,0:T(2,128)(2,1)}), bf16[4,2,26112]{2,1,0:T(2,128)(2,1)S(1)}, u32[]{:S(2)}, u32[]{:S(2)}) async-start(bf16[4,2,26112]{2,1,0:T(2,128)(2,1)} %reshape.70), calls=%async_computation | async-start | bytes 835584 | tf_op jit(solution)/shard_map/all_to_all | solution.py:270
  25.6 0.0 reduce-scatter.2.cloned.1.call-start
  25.6 0.0 copy-done.3
  25.7 6.3 %all-to-all-done = bf16[4,2,26112]{2,1,0:T(2,128)(2,1)S(1)} async-done(((bf16[4,2,26112]{2,1,0:T(2,128)(2,1)}), bf16[4,2,26112]{2,1,0:T(2,128)(2,1)S(1)}, u32[]{:S(2)}, u32[]{:S(2)}) %all-to-all-start) | async-done | bytes 417824 | tf_op jit(solution)/shard_map/all_to_all | solution.py:270
  32.0 7.9 %reshape.71 = bf16[2048,1,3,2,17]{4,3,2,1,0:T(2,128)(2,1)} reshape(bf16[4,2,26112]{2,1,0:T(2,128)(2,1)S(1)} %all-to-all-done) | data formatting | bytes 835584
  39.9 7.4 %copy.25 = bf16[1,3,2,17,4,512]{5,4,3,1,2,0:T(4,128)(2,1)S(1)} copy(bf16[1,3,2,17,4,512]{3,2,1,5,4,0:T(2,128)(2,1)} %bitcast.71) | data formatting | bytes 835584 | tf_op jit(solution)/shard_map/all_to_all | solution.py:270
  47.3 0.0 copy-start.1
  47.3 0.0 copy-start.4
  47.3 0.0 copy-start.2
  47.3 0.5 fusion.4
  47.8 0.1 fusion.9
  47.9 0.1 fusion.10
  47.9 0.0 copy-done
  47.9 0.5 fusion
  48.4 0.7 copy.65
  49.0 0.0 reduce-scatter.2.cloned.1.call-update
  49.1 0.0 copy-done.1
  49.1 0.6 copy.27
  49.7 0.0 copy-done.4
  49.7 0.7 copy.28.cycles_ref
  50.5 0.0 copy-done.2
  50.5 0.6 copy.66
  51.1 26.8 %reduce-scatter.2.cloned.1.call-done = f32[1,2,1,17,128]{4,3,1,2,0:T(8,128)} async-done(((f32[4,2,1,17,128]{4,3,1,2,0:T(8,128)}), f32[1,2,1,17,128]{4,3,1,2,0:T(8,128)}) %reduce-scatter.2.cloned.1.call-update) | async-done | bytes 17424 | tf_op jit(solution)/shard_map/reduce_scatter | solution.py:280
  77.9 1.3 %pad.4.coeff_ref = f32[2,24,128]{2,1,0:T(8,128)} pad(f32[2,17,128]{2,1,0:T(8,128)} %bitcast.81, f32[]{:T(128)} %constant.10.clone.1), padding=0_0x0_7x0_0 | pad | bytes 41988 | tf_op jit(solution)/shard_map/jit(_pad)/pad | solution.py:286
  79.3 2.9 %shard_map.109 = bf16[512,128]{1,0:T(8,128)(2,1)} custom-call(f32[2,24,128]{2,1,0:T(8,128)} %pad.4.coeff_ref, f32[2,2,24,128]{3,2,1,0:T(8,128)} %constant.11.clone.psi_ref, s32[256,128]{1,0:T(8,128)} %bitcast.74, s32[128,3]{1,0:T(8,128)} %copy.28.cycles_ref), custom_call_target="tpu_custom_call" | custom-call | tf_op jit(solution)/shard_map/pallas_call | solution.py:288
  82.2 21.7 %shard_map.110 = bf16[128,4,128]{2,1,0:T(4,128)(2,1)} custom-call(bf16[128,4,128]{2,1,0:T(4,128)(2,1)} %bitcast.76), custom_call_target="tpu_custom_call" | custom-call | tf_op jit(solution)/shard_map/pallas_call | solution.py:294
  103.9 4.4 %shard_map.111 = f32[1,4096]{1,0:T(1,128)} custom-call(s32[1]{0:T(128)} %bitcast.8.owner_ref, bf16[512,128]{1,0:T(8,128)(2,1)} %bitcast.77, s32[256,128]{1,0:T(8,128)} %bitcast.75, s32[1,128]{1,0:T(1,128)} %bitcast.82, s32[1,4096]{1,0:T(1,128)} %block_ref.1, s32[1,4096]{1,0:T(1,128)} %phi_ref.1, s32[1,4096]{1,0:T(1,128)} %psi_ref.2, f32[2,4096]{1,0:T(2,128)} %bitcast.80), custom_call_target="tpu_custom_call" | custom-call | tf_op jit(solution)/shard_map/pallas_call | solution.py:302
  (2 shorter events, 0.0 us)
Async XLA Ops:
  6.5 41.4 %copy-start = (bf16[1,17,512,128]{3,2,1,0:T(8,128)(2,1)S(1)}, bf16[1,17,512,128]{3,2,1,0:T(8,128)(2,1)}, u32[]{:S(2)}) copy-start(bf16[1,17,512,128]{3,2,1,0:T(8,128)(2,1)} %param.13) | copy-start | bytes 6684676
  14.5 11.2 %copy-start.3 = (f32[3,2,1,512]{3,2,1,0:T(1,128)S(1)}, f32[3,2,1,512]{3,2,1,0:T(1,128)}, u32[]{:S(2)}) copy-start(f32[3,2,1,512]{3,2,1,0:T(1,128)} %param.11) | copy-start | bytes 36868
  20.8 11.2 %all-to-all-start = ((bf16[4,2,26112]{2,1,0:T(2,128)(2,1)}), bf16[4,2,26112]{2,1,0:T(2,128)(2,1)S(1)}, u32[]{:S(2)}, u32[]{:S(2)}) async-start(bf16[4,2,26112]{2,1,0:T(2,128)(2,1)} %reshape.70), calls=%async_computation | async-start | bytes 835584 | tf_op jit(solution)/shard_map/all_to_all | solution.py:270
  25.6 52.3 %reduce-scatter.2.cloned.1.call-start = ((), (), s32[]{:S(2)}) async-start(), calls=%async_computation.2 | async-start | bytes 122880 | tf_op jit(solution)/shard_map/reduce_scatter | solution.py:280
  47.3 1.8 %copy-start.1 = (s32[1,128,128,2]{2,3,1,0:T(2,128)S(1)}, s32[1,128,128,2]{2,3,1,0:T(2,128)}, u32[]{:S(2)}) copy-start(s32[1,128,128,2]{2,3,1,0:T(2,128)} %param.16) | copy-start | bytes 393220
  47.3 2.4 %copy-start.4 = (s32[128,3]{0,1:T(4,128)S(1)}, s32[128,3]{0,1:T(4,128)}, u32[]{:S(2)}) copy-start(s32[128,3]{0,1:T(4,128)} %param.15) | copy-start | bytes 4612
  47.3 3.2 %copy-start.2 = (f32[2,1,4096]{2,1,0:T(1,128)S(1)}, f32[2,1,4096]{2,1,0:T(1,128)}, u32[]{:S(2)}) copy-start(f32[2,1,4096]{2,1,0:T(1,128)} %param.20) | copy-start | bytes 98308
Sparse Core Ops, SparseCore 0:
  49.2 28.7 reduce-scatter.1

commit v2 on v1

--- a/solution.py
+++ b/solution.py
@@ -17,7 +17,7 @@
 BANDS = 128
 LISTED = 8
 ROWS = 4
-ORDERS_PAD = 24
+ORDERS_PAD = 40
 CHUNK = 512
 UNLISTED = 200.0
 MESH = pl.DeviceIdType.MESH
@@ -28,11 +28,11 @@
     cells = np.arange(128) % NPSI
     angle = 2.0 * math.pi / NPSI * ((orders[:, None] * cells[None, :]) % NPSI)
     cos_psi, sin_psi = np.cos(angle), np.sin(angle)
-    table = np.zeros((2, 2, ORDERS_PAD, 128), np.float32)
-    table[0, 0, :MPRIME] = cos_psi
-    table[0, 1, :MPRIME] = -sin_psi
-    table[1, 0, :MPRIME] = sin_psi
-    table[1, 1, :MPRIME] = cos_psi
+    table = np.zeros((2, ORDERS_PAD, 128), np.float32)
+    table[0, 0 : 2 * MPRIME : 2] = cos_psi
+    table[0, 1 : 2 * MPRIME : 2] = -sin_psi
+    table[1, 0 : 2 * MPRIME : 2] = sin_psi
+    table[1, 1 : 2 * MPRIME : 2] = cos_psi
     return table
 
 
@@ -87,21 +87,24 @@
 def choose_payload(coeff, psi_table, codes, cycles):
     highest = lax.Precision.HIGHEST
     rank = list_ranks(codes)
-    both = jnp.concatenate([cycles, cycles], 0)
+    entries = codes.shape[0]
+    source = ones_where(iota((entries, BANDS), 0) // 2 == iota((entries, BANDS), 1))
+    both = lax.dot_general(
+        source,
+        cycles.astype(jnp.float32).astype(jnp.bfloat16),
+        (((1,), (1,)), ((), ())),
+        preferred_element_type=jnp.float32,
+    )
     slot = lax.shift_right_arithmetic(codes, 12)
     cycle = jnp.where(slot == 0, both[:, 0:1], jnp.where(slot == 1, both[:, 1:2], both[:, 2:3]))
     width = BANDS * ROWS
     spread = ones_where(iota((BANDS, width), 1) // ROWS == iota((BANDS, width), 0))
     rank_wide = dot(rank.astype(jnp.bfloat16), spread)
-    cycle_wide = dot(cycle.astype(jnp.float32).astype(jnp.bfloat16), spread)
+    cycle_wide = dot(cycle.astype(jnp.bfloat16), spread)
     place = iota((1, width), 1) % ROWS
     half = place % 2
     lane_group = iota((BANDS, 128), 1) // NPSI
-    waves = [
-        dot_rows(coeff[0], psi_table[part, 0], highest)
-        + dot_rows(coeff[1], psi_table[part, 1], highest)
-        for part in range(2)
-    ]
+    waves = [dot_rows(coeff, psi_table[part], highest) for part in range(2)]
     row_cycle = iota((128, width), 0).astype(jnp.float32)
     total = None
     for group in range(4):
@@ -123,8 +126,7 @@
     rank_col = jnp.sum(jnp.where(mine, rank, 0.0), 1, keepdims=True)
     start = jnp.bitwise_and(codes, NPHI - 1).astype(jnp.float32)
     start_col = jnp.sum(jnp.where(mine, start, 0.0), 1, keepdims=True)
-    place = iota((entries, 128), 0)
-    name = (place % BANDS * 2 + place // BANDS + 1).astype(jnp.float32)
+    name = (iota((entries, 128), 0) + 1).astype(jnp.float32)
     lanes = iota((entries, 128), 1).astype(jnp.float32)
     picked = rank_col == lanes
     name_row = jnp.sum(jnp.where(picked, name, 0.0), 0, keepdims=True) - 1.0
@@ -172,8 +174,96 @@
     return jnp.sum(weight * row, 0, keepdims=True)
 
 
+def coeff_kernel(
+    dets,
+    beam_ref,
+    sky_ref,
+    panel_ref,
+    out_ref,
+    beams,
+    panel,
+    part,
+    parts,
+    own_sem,
+    send_sem,
+    recv_sem,
+):
+    me = lax.axis_index("det")
+    comps, span = beams.shape[1], beams.shape[4]
+    rows = 2 * dets
+    peers = [lax.rem(me + step, dets) for step in range(dets)]
+    barrier = pltpu.get_barrier_semaphore()
+    for step in range(1, dets):
+        pl.semaphore_signal(
+            barrier, inc=1, device_id={"det": peers[step]}, device_id_type=MESH
+        )
+    own_panel = pltpu.make_async_copy(panel_ref, panel, own_sem.at[0])
+    own_panel.start()
+
+    def columns(det):
+        return beam_ref.at[:, :, :, pl.ds(pl.multiple_of(det * span, span), span)]
+
+    own_beams = pltpu.make_async_copy(columns(me), beams.at[me], own_sem.at[1])
+    own_beams.start()
+    pl.semaphore_wait(barrier, dets - 1)
+
+    def remote(stage, step, source, target):
+        return pltpu.make_async_remote_copy(
+            src_ref=source,
+            dst_ref=target,
+            send_sem=send_sem.at[stage, step],
+            recv_sem=recv_sem.at[stage, step],
+            device_id={"det": peers[step]},
+            device_id_type=MESH,
+        )
+
+    sends = [
+        remote(0, step, columns(peers[step]), beams.at[me]) for step in range(1, dets)
+    ]
+    for copy in sends:
+        copy.start()
+    own_panel.wait()
+    own_beams.wait()
+    for copy in sends:
+        copy.wait()
+    real_row = iota((rows, span), 0) % 2 == 0
+    direct, crossed = [], []
+    for comp in range(comps):
+        first = jnp.broadcast_to(sky_ref[2 * comp], (rows, span))
+        direct.append(jnp.where(real_row, first, -first))
+        crossed.append(jnp.broadcast_to(sky_ref[2 * comp + 1], (rows, span)))
+
+    def one_order(order, carry):
+        mixed = jnp.zeros((rows, span), jnp.float32)
+        for comp in range(comps):
+            values = jnp.concatenate(
+                [beams[det, comp, order].astype(jnp.float32) for det in range(dets)], 0
+            )
+            swapped = jnp.where(
+                real_row, pltpu.roll(values, rows - 1, 0), pltpu.roll(values, 1, 0)
+            )
+            mixed = mixed + direct[comp] * values + crossed[comp] * swapped
+        sums = dot(mixed.astype(jnp.bfloat16), panel[order])
+        for det in range(dets):
+            part[det, order] = sums[2 * det : 2 * det + 2]
+        return carry
+
+    lax.fori_loop(0, MPRIME, one_order, 0)
+    sends = [remote(1, step, part.at[peers[step]], parts.at[me]) for step in range(1, dets)]
+    for copy in sends:
+        copy.start()
+    for copy in sends:
+        copy.wait()
+    out_ref[...] = jnp.zeros_like(out_ref)
+    for order in range(MPRIME):
+        total = part[me, order]
+        for step in range(1, dets):
+            total = total + parts[peers[step], order]
+        out_ref[2 * order : 2 * order + 2, :] = total
+
+
 def payload_kernel(coeff_ref, psi_ref, codes_ref, cycles_ref, out_ref):
-    out_ref[...] = choose_payload(coeff_ref, psi_ref, codes_ref[...], cycles_ref[...])
+    out_ref[...] = choose_payload(coeff_ref[...], psi_ref, codes_ref[...], cycles_ref[...])
 
 
 def exchange_kernel(bands, src_ref, dst_ref, send_sem, recv_sem, own_sem):
@@ -242,8 +332,8 @@
             block_ref[:, part],
             phi_ref[:, part],
             psi_ref[:, part],
-            frac_ref[0:1, part],
-            frac_ref[1:2, part],
+            frac_ref[0, :, part],
+            frac_ref[1, :, part],
         )
 
 
@@ -263,34 +353,40 @@
     sample_psi,
     sample_frac,
 ):
-    highest = lax.Precision.HIGHEST
     orders_all = m_values.shape[0]
     scale = 2.0 / math.sqrt(orders_all * MPRIME)
     own_band = lax.axis_index("band")
-    beams = lax.all_to_all(beam_coeffs, "det", split_axis=4, concat_axis=0, tiled=True).astype(
-        jnp.float32
-    )
-    mix_real = jnp.einsum(
-        "cmk,dcnk->dmnk", sky_coeffs[:, 0], beams[:, :, 0], precision=highest
-    ) + jnp.einsum("cmk,dcnk->dmnk", sky_coeffs[:, 1], beams[:, :, 1], precision=highest)
-    mix_imag = jnp.einsum(
-        "cmk,dcnk->dmnk", sky_coeffs[:, 1], beams[:, :, 0], precision=highest
-    ) - jnp.einsum("cmk,dcnk->dmnk", sky_coeffs[:, 0], beams[:, :, 1], precision=highest)
-    mixed = jnp.stack([mix_real, mix_imag], 1).astype(jnp.bfloat16)
-    coeff = lax.psum_scatter(
-        jnp.einsum("dsmnk,mnkr->dsmnr", mixed, wigner_panel, preferred_element_type=jnp.float32),
-        "det",
-        scatter_dimension=0,
-        tiled=True,
-    )[0]
-    coeff = jnp.pad(coeff[:, 0], ((0, 0), (0, ORDERS_PAD - MPRIME), (0, 0)))
-    codes = jnp.transpose(send_lists[0], (2, 0, 1)).reshape(2 * BANDS, BANDS)
+    comps, span = sky_coeffs.shape[0], sky_coeffs.shape[3]
+    cycles = wigner_panel.shape[3]
+    beams = jnp.transpose(beam_coeffs[0], (0, 2, 1, 3))
+    dets = beams.shape[3] // span
+    coeff = pl.pallas_call(
+        functools.partial(coeff_kernel, dets),
+        out_shape=jax.ShapeDtypeStruct((ORDERS_PAD, cycles), jnp.float32),
+        in_specs=[
+            pl.BlockSpec(memory_space=pl.ANY),
+            pl.BlockSpec(memory_space=pltpu.VMEM),
+            pl.BlockSpec(memory_space=pl.ANY),
+        ],
+        out_specs=vmem_specs(1)[0],
+        scratch_shapes=[
+            pltpu.VMEM((dets, comps, MPRIME, 2, span), jnp.bfloat16),
+            pltpu.VMEM((MPRIME, span, cycles), jnp.bfloat16),
+            pltpu.VMEM((dets, MPRIME, 2, cycles), jnp.float32),
+            pltpu.VMEM((dets, MPRIME, 2, cycles), jnp.float32),
+            pltpu.SemaphoreType.DMA((2,)),
+            pltpu.SemaphoreType.DMA((2, dets)),
+            pltpu.SemaphoreType.DMA((2, dets)),
+        ],
+        compiler_params=pltpu.CompilerParams(collective_id=1, has_side_effects=True),
+    )(beams, sky_coeffs.reshape(2 * comps, 1, span), wigner_panel[0])
+    codes = jnp.transpose(send_lists[0], (0, 2, 1)).reshape(2 * BANDS, BANDS)
     payload = pl.pallas_call(
         payload_kernel,
         out_shape=jax.ShapeDtypeStruct((BANDS * ROWS, 128), jnp.bfloat16),
         in_specs=vmem_specs(4),
         out_specs=vmem_specs(1)[0],
-    )(coeff, jnp.asarray(psi_matrices()), codes, cycle_table)
+    )(coeff, jnp.asarray(psi_matrices()), codes, cycle_table.T)
     received = pl.pallas_call(
         functools.partial(exchange_kernel, BANDS),
         out_shape=jax.ShapeDtypeStruct((BANDS, ROWS, 128), jnp.bfloat16),
@@ -312,7 +408,7 @@
         sample_block,
         sample_phi,
         sample_psi,
-        sample_frac[:, 0],
+        sample_frac,
     )
 
 

time: 116 us -> 51.8 us (0.45)
  local copies, waits for them, and re-layouts: 33.6 us -> 0 us
  waiting for transfers between devices: 33.2 us -> 0 us
  Pallas kernels: 29 us -> 51.5 us
  between operations: 13.5 us -> 0.02 us
  starting transfers between devices: 4.83 us -> 0 us
    reduce_scatter x1 -> x0, waiting for transfers between devices: 26.8 us -> none  [per_device(): lax.psum_scatter(jnp.einsum('dsmnk,mnkr->dsmnr', mixed, wigner_panel, pre...]
    unnamed x16 -> x0, local copies, waits for them, and re-layouts: 23.5 us -> none
    pallas_call x0 -> x1, Pallas kernels: none -> 16.2 us  [per_device(): pl.pallas_call(functools.partial(coeff_kernel, dets), out_shape=jax.Shape...]
    all_to_all x1 -> x0, local copies, waits for them, and re-layouts: 7.39 us -> none  [per_device(): lax.all_to_all(beam_coeffs, 'det', split_axis=4, concat_axis=0, tiled=True)]
    pallas_call x1, Pallas kernels: 21.7 us -> 28.1 us  [per_device(): pl.pallas_call(functools.partial(exchange_kernel, BANDS), out_shape=jax.S...]
    all_to_all x1 -> x0, waiting for transfers between devices: 6.34 us -> none  [per_device(): lax.all_to_all(beam_coeffs, 'det', split_axis=4, concat_axis=0, tiled=True)]
    all_to_all x1 -> x0, starting transfers between devices: 4.83 us -> none  [per_device(): lax.all_to_all(beam_coeffs, 'det', split_axis=4, concat_axis=0, tiled=True)]
    pad x1 -> x0, local copies, waits for them, and re-layouts: 1.34 us -> none  [per_device(): coeff = jnp.pad(coeff[:, 0], ((0, 0), (0, ORDERS_PAD - MPRIME), (0, 0)))]
  transfers between devices with their start and end apart: 2 -> 0, of which waited for: 2 -> 0; matrix products, arithmetic and copies ran while one was open for 2% -> 0% of each run, Pallas kernels for 0% -> 0%
where the time goes in v2:
time: 51.8 us; the launch traced here: 51.5 us
  Pallas kernels  51.5 us (99%)
    pallas_call x1, Pallas kernels, per_device(): pl.pallas_call(functools.partial(exchange_kernel, BANDS), out_shape=jax.S...  28.1 us
    pallas_call x1, Pallas kernels, per_device(): pl.pallas_call(functools.partial(coeff_kernel, dets), out_shape=jax.Shape...  16.2 us
    pallas_call x1, Pallas kernels, per_device(): pl.pallas_call(functools.partial(samples_kernel, scale), out_shape=jax.Sh...  4.42 us
    pallas_call x1, Pallas kernels, per_device(): pl.pallas_call(payload_kernel, out_shape=jax.ShapeDtypeStruct((BANDS * RO...  2.83 us

profile of v2, /device:TPU:1, one launch (start us, length us, event | category | flops | bytes accessed | tf_op | source)
XLA Modules:
  0.0 51.5 jit_solution(14726759063317591846)
XLA Ops:
  0.0 16.2 %shard_map.109.coeff_ref = f32[40,128]{1,0:T(8,128)} custom-call(bf16[3,17,2,2048]{3,2,1,0:T(2,128)(2,1)} %bitcast.20, f32[6,1,512]{2,1,0:T(1,128)} %bitcast.21, bf16[17,512,128]{2,1,0:T(8,128)(2,1)} %bitcast.15), custom_call_target="tpu_custom_call" | custom-call | tf_op jit(solution)/shard_map/pallas_call | solution.py:363
  16.2 2.8 %shard_map.110 = bf16[512,128]{1,0:T(8,128)(2,1)} custom-call(f32[40,128]{1,0:T(8,128)} %shard_map.109.coeff_ref, f32[2,40,128]{2,1,0:T(8,128)} %constant.8.clone.psi_ref, s32[256,128]{1,0:T(8,128)} %bitcast.17, s32[3,128]{1,0:T(4,128)} %bitcast.22), custom_call_target="tpu_custom_call" | custom-call | tf_op jit(solution)/shard_map/pallas_call | solution.py:384
  19.1 28.1 %shard_map.111 = bf16[128,4,128]{2,1,0:T(4,128)(2,1)} custom-call(bf16[128,4,128]{2,1,0:T(4,128)(2,1)} %bitcast.16), custom_call_target="tpu_custom_call" | custom-call | tf_op jit(solution)/shard_map/pallas_call | solution.py:390
  47.1 4.4 %shard_map.112 = f32[1,4096]{1,0:T(1,128)} custom-call(s32[1]{0:T(128)} %bitcast.owner_ref, bf16[512,128]{1,0:T(8,128)(2,1)} %bitcast.19, s32[256,128]{1,0:T(8,128)} %bitcast.18, s32[1,128]{1,0:T(1,128)} %bitcast.23, s32[1,4096]{1,0:T(1,128)} %block_ref.1, s32[1,4096]{1,0:T(1,128)} %phi_ref.1, s32[1,4096]{1,0:T(1,128)} %psi_ref.2, f32[2,1,4096]{2,1,0:T(1,128)} %frac_ref.1), custom_call_target="tpu_custom_call" | custom-call | tf_op jit(solution)/shard_map/pallas_call | solution.py:398

commit v3 on v2

--- a/solution.py
+++ b/solution.py
@@ -84,8 +84,11 @@
     return jnp.where(listed, rank, UNLISTED)
 
 
-def choose_payload(coeff, psi_table, codes, cycles):
-    highest = lax.Precision.HIGHEST
+def payload_places():
+    return iota((1, BANDS * ROWS), 1) % ROWS
+
+
+def choose_cycles(codes, cycles):
     rank = list_ranks(codes)
     entries = codes.shape[0]
     source = ones_where(iota((entries, BANDS), 0) // 2 == iota((entries, BANDS), 1))
@@ -101,19 +104,28 @@
     spread = ones_where(iota((BANDS, width), 1) // ROWS == iota((BANDS, width), 0))
     rank_wide = dot(rank.astype(jnp.bfloat16), spread)
     cycle_wide = dot(cycle.astype(jnp.bfloat16), spread)
-    place = iota((1, width), 1) % ROWS
-    half = place % 2
-    lane_group = iota((BANDS, 128), 1) // NPSI
-    waves = [dot_rows(coeff, psi_table[part], highest) for part in range(2)]
-    row_cycle = iota((128, width), 0).astype(jnp.float32)
-    total = None
+    half = payload_places() % 2
+    chosen = []
     for group in range(4):
         wanted = (4 * half + group).astype(jnp.float32)
-        chosen = jnp.sum(jnp.where(rank_wide == wanted, cycle_wide, 0.0), 0, keepdims=True)
-        for part in range(2):
-            target = jnp.where(place // 2 == part, chosen, -1.0)
+        chosen.append(
+            jnp.sum(jnp.where(rank_wide == wanted, cycle_wide, 0.0), 0, keepdims=True)
+        )
+    return chosen
+
+
+def gather_payload(coeff, psi_table, chosen):
+    width = BANDS * ROWS
+    lane_group = iota((BANDS, 128), 1) // NPSI
+    row_cycle = iota((128, width), 0).astype(jnp.float32)
+    part_of = payload_places() // 2
+    total = None
+    for part in range(2):
+        waves = dot_rows(coeff, psi_table[part], lax.Precision.HIGHEST)
+        for group in range(4):
+            target = jnp.where(part_of == part, chosen[group], -1.0)
             hot = ones_where(row_cycle == target)
-            piece = jnp.where(lane_group == group, waves[part], 0.0).astype(jnp.bfloat16)
+            piece = jnp.where(lane_group == group, waves, 0.0).astype(jnp.bfloat16)
             term = dot_rows(hot, piece)
             total = term if total is None else total + term
     return total.astype(jnp.bfloat16)
@@ -174,29 +186,83 @@
     return jnp.sum(weight * row, 0, keepdims=True)
 
 
-def coeff_kernel(
+def signal_kernel(
+    bands,
     dets,
+    scale,
     beam_ref,
-    sky_ref,
     panel_ref,
+    sky_in,
+    psi_in,
+    codes_in,
+    cycles_in,
+    orders_in,
+    block_in,
+    phi_in,
+    cell_in,
+    frac_in,
     out_ref,
     beams,
     panel,
     part,
     parts,
+    coeff,
+    chosen_ref,
+    keys_ref,
+    cos_ref,
+    sin_ref,
+    payload,
+    received,
+    sky_ref,
+    psi_ref,
+    codes_ref,
+    cycles_ref,
+    orders_ref,
+    block_ref,
+    phi_ref,
+    cell_ref,
+    frac_ref,
+    in_sem,
     own_sem,
     send_sem,
     recv_sem,
+    out_sem,
+    all_sem,
 ):
     me = lax.axis_index("det")
+    owner = lax.axis_index("band")
     comps, span = beams.shape[1], beams.shape[4]
     rows = 2 * dets
     peers = [lax.rem(me + step, dets) for step in range(dets)]
     barrier = pltpu.get_barrier_semaphore()
+
+    def greet(step, carry):
+        peer = lax.rem(owner + step, bands)
+        pl.semaphore_signal(barrier, inc=1, device_id={"band": peer}, device_id_type=MESH)
+        return carry
+
+    lax.fori_loop(1, bands, greet, 0)
     for step in range(1, dets):
         pl.semaphore_signal(
             barrier, inc=1, device_id={"det": peers[step]}, device_id_type=MESH
         )
+    staged = [
+        (codes_in, codes_ref),
+        (cycles_in, cycles_ref),
+        (orders_in, orders_ref),
+        (sky_in, sky_ref),
+        (psi_in, psi_ref),
+        (block_in, block_ref),
+        (phi_in, phi_ref),
+        (cell_in, cell_ref),
+        (frac_in, frac_ref),
+    ]
+    loads = [
+        pltpu.make_async_copy(source, target, in_sem.at[place])
+        for place, (source, target) in enumerate(staged)
+    ]
+    for load in loads:
+        load.start()
     own_panel = pltpu.make_async_copy(panel_ref, panel, own_sem.at[0])
     own_panel.start()
 
@@ -205,7 +271,13 @@
 
     own_beams = pltpu.make_async_copy(columns(me), beams.at[me], own_sem.at[1])
     own_beams.start()
-    pl.semaphore_wait(barrier, dets - 1)
+    for load in loads:
+        load.wait()
+    for group, row in enumerate(choose_cycles(codes_ref[...], cycles_ref[...])):
+        chosen_ref[group : group + 1, :] = row
+    keys, places = own_blocks(codes_ref[...], owner)
+    keys_ref[...] = jnp.broadcast_to(keys, keys_ref.shape)
+    pl.semaphore_wait(barrier, bands - 1 + dets - 1)
 
     def remote(stage, step, source, target):
         return pltpu.make_async_remote_copy(
@@ -222,6 +294,9 @@
     ]
     for copy in sends:
         copy.start()
+    turns = places * orders_ref[...]
+    cos_ref[...] = cosine_of_turns(turns).astype(jnp.bfloat16)
+    sin_ref[...] = cosine_of_turns(turns + NPHI // 4).astype(jnp.bfloat16)
     own_panel.wait()
     own_beams.wait()
     for copy in sends:
@@ -254,39 +329,24 @@
         copy.start()
     for copy in sends:
         copy.wait()
-    out_ref[...] = jnp.zeros_like(out_ref)
+    coeff[...] = jnp.zeros_like(coeff)
     for order in range(MPRIME):
         total = part[me, order]
         for step in range(1, dets):
             total = total + parts[peers[step], order]
-        out_ref[2 * order : 2 * order + 2, :] = total
-
-
-def payload_kernel(coeff_ref, psi_ref, codes_ref, cycles_ref, out_ref):
-    out_ref[...] = choose_payload(coeff_ref[...], psi_ref, codes_ref[...], cycles_ref[...])
-
-
-def exchange_kernel(bands, src_ref, dst_ref, send_sem, recv_sem, own_sem):
-    me = lax.axis_index("band")
-    barrier = pltpu.get_barrier_semaphore()
-
-    def greet(step, carry):
-        peer = lax.rem(me + step, bands)
-        pl.semaphore_signal(barrier, inc=1, device_id={"band": peer}, device_id_type=MESH)
-        return carry
-
-    lax.fori_loop(1, bands, greet, 0)
-    own = pltpu.make_async_copy(src_ref.at[me], dst_ref.at[me], own_sem)
+        coeff[2 * order : 2 * order + 2, :] = total
+    chosen = [chosen_ref[group : group + 1, :] for group in range(4)]
+    payload[...] = gather_payload(coeff[...], psi_ref, chosen).reshape(payload.shape)
+    own = pltpu.make_async_copy(payload.at[owner], received.at[owner], own_sem.at[2])
     own.start()
-    pl.semaphore_wait(barrier, bands - 1)
 
     def send(step, carry):
-        peer = lax.rem(me + step, bands)
+        peer = lax.rem(owner + step, bands)
         pltpu.make_async_remote_copy(
-            src_ref=src_ref.at[peer],
-            dst_ref=dst_ref.at[me],
-            send_sem=send_sem,
-            recv_sem=recv_sem,
+            src_ref=payload.at[peer],
+            dst_ref=received.at[owner],
+            send_sem=out_sem,
+            recv_sem=all_sem,
             device_id={"band": peer},
             device_id_type=MESH,
         ).start()
@@ -296,49 +356,30 @@
     own.wait()
     others = pl.ds(0, bands - 1)
     everything = pltpu.make_async_remote_copy(
-        src_ref=src_ref.at[others],
-        dst_ref=dst_ref.at[others],
-        send_sem=send_sem,
-        recv_sem=recv_sem,
-        device_id={"band": me},
+        src_ref=payload.at[others],
+        dst_ref=received.at[others],
+        send_sem=out_sem,
+        recv_sem=all_sem,
+        device_id={"band": owner},
         device_id_type=MESH,
     )
-    everything.wait_send()
     everything.wait_recv()
-
-
-def samples_kernel(
-    scale,
-    owner_ref,
-    received_ref,
-    codes_ref,
-    orders_ref,
-    block_ref,
-    phi_ref,
-    psi_ref,
-    frac_ref,
-    out_ref,
-):
-    keys, columns = own_blocks(codes_ref[...], owner_ref[0])
-    turns = columns * orders_ref[...]
-    cos_phase = cosine_of_turns(turns).astype(jnp.bfloat16)
-    sin_phase = cosine_of_turns(turns + NPHI // 4).astype(jnp.bfloat16)
-    cells = block_cells(received_ref[...], cos_phase, sin_phase, scale)
+    cells = block_cells(
+        received[...].reshape(BANDS * ROWS, 128), cos_ref, sin_ref, scale
+    )
+    keys = keys_ref[:, 0:1]
     for first in range(0, block_ref.shape[1], CHUNK):
-        part = slice(first, first + CHUNK)
-        out_ref[:, part] = blend(
+        piece = slice(first, first + CHUNK)
+        out_ref[:, piece] = blend(
             cells,
             keys,
-            block_ref[:, part],
-            phi_ref[:, part],
-            psi_ref[:, part],
-            frac_ref[0, :, part],
-            frac_ref[1, :, part],
+            block_ref[:, piece],
+            phi_ref[:, piece],
+            cell_ref[:, piece],
+            frac_ref[0, :, piece],
+            frac_ref[1, :, piece],
         )
-
-
-def vmem_specs(count):
-    return [pl.BlockSpec(memory_space=pltpu.VMEM)] * count
+    everything.wait_send()
 
 
 def per_device(
@@ -355,61 +396,52 @@
 ):
     orders_all = m_values.shape[0]
     scale = 2.0 / math.sqrt(orders_all * MPRIME)
-    own_band = lax.axis_index("band")
     comps, span = sky_coeffs.shape[0], sky_coeffs.shape[3]
     cycles = wigner_panel.shape[3]
     beams = jnp.transpose(beam_coeffs[0], (0, 2, 1, 3))
     dets = beams.shape[3] // span
-    coeff = pl.pallas_call(
-        functools.partial(coeff_kernel, dets),
-        out_shape=jax.ShapeDtypeStruct((ORDERS_PAD, cycles), jnp.float32),
-        in_specs=[
-            pl.BlockSpec(memory_space=pl.ANY),
-            pl.BlockSpec(memory_space=pltpu.VMEM),
-            pl.BlockSpec(memory_space=pl.ANY),
-        ],
-        out_specs=vmem_specs(1)[0],
+    samples = sample_block.shape[1]
+    codes = jnp.transpose(send_lists[0], (0, 2, 1)).reshape(2 * BANDS, BANDS)
+    small = [
+        sky_coeffs.reshape(2 * comps, 1, span),
+        jnp.asarray(psi_matrices()),
+        codes,
+        cycle_table.T,
+        m_values.reshape(1, orders_all),
+        sample_block,
+        sample_phi,
+        sample_psi,
+        sample_frac,
+    ]
+    return pl.pallas_call(
+        functools.partial(signal_kernel, BANDS, dets, scale),
+        out_shape=jax.ShapeDtypeStruct((1, samples), jnp.float32),
+        in_specs=[pl.BlockSpec(memory_space=pl.ANY)] * (2 + len(small)),
+        out_specs=pl.BlockSpec(memory_space=pltpu.VMEM),
         scratch_shapes=[
             pltpu.VMEM((dets, comps, MPRIME, 2, span), jnp.bfloat16),
             pltpu.VMEM((MPRIME, span, cycles), jnp.bfloat16),
             pltpu.VMEM((dets, MPRIME, 2, cycles), jnp.float32),
             pltpu.VMEM((dets, MPRIME, 2, cycles), jnp.float32),
-            pltpu.SemaphoreType.DMA((2,)),
+            pltpu.VMEM((ORDERS_PAD, cycles), jnp.float32),
+            pltpu.VMEM((4, BANDS * ROWS), jnp.float32),
+            pltpu.VMEM((LISTED * NPSI, 128), jnp.int32),
+            pltpu.VMEM((LISTED * BLOCK_PHI, orders_all), jnp.bfloat16),
+            pltpu.VMEM((LISTED * BLOCK_PHI, orders_all), jnp.bfloat16),
+            pltpu.VMEM((BANDS, ROWS, 128), jnp.bfloat16),
+            pltpu.VMEM((BANDS, ROWS, 128), jnp.bfloat16),
+        ]
+        + [pltpu.VMEM(array.shape, array.dtype) for array in small]
+        + [
+            pltpu.SemaphoreType.DMA((len(small),)),
+            pltpu.SemaphoreType.DMA((3,)),
             pltpu.SemaphoreType.DMA((2, dets)),
             pltpu.SemaphoreType.DMA((2, dets)),
+            pltpu.SemaphoreType.DMA,
+            pltpu.SemaphoreType.DMA,
         ],
-        compiler_params=pltpu.CompilerParams(collective_id=1, has_side_effects=True),
-    )(beams, sky_coeffs.reshape(2 * comps, 1, span), wigner_panel[0])
-    codes = jnp.transpose(send_lists[0], (0, 2, 1)).reshape(2 * BANDS, BANDS)
-    payload = pl.pallas_call(
-        payload_kernel,
-        out_shape=jax.ShapeDtypeStruct((BANDS * ROWS, 128), jnp.bfloat16),
-        in_specs=vmem_specs(4),
-        out_specs=vmem_specs(1)[0],
-    )(coeff, jnp.asarray(psi_matrices()), codes, cycle_table.T)
-    received = pl.pallas_call(
-        functools.partial(exchange_kernel, BANDS),
-        out_shape=jax.ShapeDtypeStruct((BANDS, ROWS, 128), jnp.bfloat16),
-        in_specs=vmem_specs(1),
-        out_specs=vmem_specs(1)[0],
-        scratch_shapes=[pltpu.SemaphoreType.DMA] * 3,
         compiler_params=pltpu.CompilerParams(collective_id=0, has_side_effects=True),
-    )(payload.reshape(BANDS, ROWS, 128))
-    return pl.pallas_call(
-        functools.partial(samples_kernel, scale),
-        out_shape=jax.ShapeDtypeStruct(sample_block.shape, jnp.float32),
-        in_specs=[pl.BlockSpec(memory_space=pltpu.SMEM)] + vmem_specs(7),
-        out_specs=vmem_specs(1)[0],
-    )(
-        own_band.reshape(1),
-        received.reshape(BANDS * ROWS, 128),
-        codes,
-        m_values.reshape(1, orders_all),
-        sample_block,
-        sample_phi,
-        sample_psi,
-        sample_frac,
-    )
+    )(beams, wigner_panel[0], *small)
 
 
 def solution(mesh):

time: 51.8 us -> 44.3 us (0.86)
  Pallas kernels: 51.5 us -> 42.8 us
  local copies, waits for them, and re-layouts: 0 us -> 1.32 us
    pallas_call x4 -> x1, Pallas kernels: 51.5 us -> 42.8 us  [per_device(): pl.pallas_call(functools.partial(signal_kernel, BANDS, dets, scale), out_...]
    unnamed x0 -> x1, local copies, waits for them, and re-layouts: none -> 1.32 us
where the time goes in v3:
time: 44.3 us; the launch traced here: 44.1 us
  Pallas kernels  42.8 us (97%)
  local copies, waits for them, and re-layouts  1.32 us (3%)
    pallas_call x1, Pallas kernels, per_device(): pl.pallas_call(functools.partial(signal_kernel, BANDS, dets, scale), out_...  42.8 us
    unnamed x1, local copies, waits for them, and re-layouts  1.32 us

profile of v3, /device:TPU:1, one launch (start us, length us, event | category | flops | bytes accessed | tf_op | source)
XLA Modules:
  0.0 44.1 jit_solution(9540240728400338876)
XLA Ops:
  0.0 42.8 %shard_map.109 = f32[1,4096]{1,0:T(1,128)} custom-call(bf16[3,17,2,2048]{3,2,1,0:T(2,128)(2,1)} %bitcast.13, bf16[17,512,128]{2,1,0:T(8,128)(2,1)} %bitcast.12, f32[6,1,512]{2,1,0:T(1,128)} %bitcast.15, f32[2,40,128]{2,1,0:T(8,128)} %constant.2.clone.psi_in, s32[256,128]{1,0:T(8,128)} %bitcast.14, s32[3,128]{1,0:T(4,128)} %bitcast.16, s32[1,128]{1,0:T(1,128)} %bitcast.17, ...), custom_call_target="tpu_custom_call" | custom-call | tf_op jit(solution)/shard_map/pallas_call | solution.py:416
  42.8 1.3 %copy.13 = f32[1,4096]{1,0:T(1,128)} copy(f32[1,4096]{1,0:T(1,128)} %shard_map.109) | data formatting | bytes 32768

commit v4 on v3

--- a/solution.py
+++ b/solution.py
@@ -19,6 +19,8 @@
 ROWS = 4
 ORDERS_PAD = 40
 CHUNK = 512
+LINE = 16
+ORDER_CUTS = (0, 6, 12, 17)
 UNLISTED = 200.0
 MESH = pl.DeviceIdType.MESH
 
@@ -114,21 +116,25 @@
     return chosen
 
 
-def gather_payload(coeff, psi_table, chosen):
+def payload_masks(chosen):
     width = BANDS * ROWS
+    part_of = payload_places() // 2
+    rows = [
+        jnp.where(part_of == part, chosen[group], -1.0) for part in range(2) for group in range(4)
+    ]
+    targets = jnp.transpose(jnp.concatenate(rows, 0))
+    cycle = iota((width, 128), 1).astype(jnp.float32)
+    return [ones_where(cycle == targets[:, place : place + 1]) for place in range(len(rows))]
+
+
+def payload_waves(coeff, psi_table):
     lane_group = iota((BANDS, 128), 1) // NPSI
-    row_cycle = iota((128, width), 0).astype(jnp.float32)
-    part_of = payload_places() // 2
-    total = None
+    pieces = []
     for part in range(2):
         waves = dot_rows(coeff, psi_table[part], lax.Precision.HIGHEST)
         for group in range(4):
-            target = jnp.where(part_of == part, chosen[group], -1.0)
-            hot = ones_where(row_cycle == target)
-            piece = jnp.where(lane_group == group, waves, 0.0).astype(jnp.bfloat16)
-            term = dot_rows(hot, piece)
-            total = term if total is None else total + term
-    return total.astype(jnp.bfloat16)
+            pieces.append(jnp.where(lane_group == group, waves, 0.0).astype(jnp.bfloat16))
+    return jnp.concatenate(pieces, 0)
 
 
 def own_blocks(codes, owner):
@@ -174,16 +180,18 @@
     return jnp.concatenate(halves, 1)
 
 
-def blend(cells, keys, block, cell_phi, cell_psi, frac_phi, frac_psi):
-    count = block.shape[1]
+def blend_masks(keys, block, cell_psi):
     base = block * NPSI
     low = ones_where(keys == base + cell_psi)
     high = ones_where(keys == base + jnp.bitwise_and(cell_psi + 1, NPSI - 1))
-    row = (1.0 - frac_psi) * dot(cells, low) + frac_psi * dot(cells, high)
-    places = iota((BLOCK_PHI, count), 0)
+    return low, high
+
+
+def blend_weights(cell_phi, frac_phi, frac_psi):
+    places = iota((BLOCK_PHI, cell_phi.shape[1]), 0)
     weight = jnp.where(places == cell_phi, 1.0 - frac_phi, 0.0)
     weight = jnp.where(places == cell_phi + 1, frac_phi, weight)
-    return jnp.sum(weight * row, 0, keepdims=True)
+    return weight * (1.0 - frac_psi), weight * frac_psi
 
 
 def signal_kernel(
@@ -207,7 +215,11 @@
     part,
     parts,
     coeff,
-    chosen_ref,
+    hot_ref,
+    low_ref,
+    high_ref,
+    low_weight,
+    high_weight,
     keys_ref,
     cos_ref,
     sin_ref,
@@ -236,12 +248,30 @@
     peers = [lax.rem(me + step, dets) for step in range(dets)]
     barrier = pltpu.get_barrier_semaphore()
 
-    def greet(step, carry):
-        peer = lax.rem(owner + step, bands)
+    def far_first(act):
+        around = LINE // 2
+        shifts = [
+            around + (turn // 2 if turn % 2 == 0 else -(turn + 1) // 2)
+            for turn in range(bands // LINE)
+        ]
+        line = lax.rem(owner, LINE)
+        column = owner // LINE
+        for shift in [bands // (2 * LINE) + value - around for value in shifts]:
+            first = lax.rem(column + shift, bands // LINE) * LINE
+
+            def one(step, carry):
+                act(first + lax.rem(line + step, LINE))
+                return carry
+
+            if shift == 0:
+                lax.fori_loop(1, LINE, one, 0)
+            else:
+                lax.fori_loop(around, around + LINE, one, 0, unroll=4)
+
+    def greet(peer):
         pl.semaphore_signal(barrier, inc=1, device_id={"band": peer}, device_id_type=MESH)
-        return carry
-
-    lax.fori_loop(1, bands, greet, 0)
+
+    far_first(greet)
     for step in range(1, dets):
         pl.semaphore_signal(
             barrier, inc=1, device_id={"det": peers[step]}, device_id_type=MESH
@@ -266,15 +296,17 @@
     own_panel = pltpu.make_async_copy(panel_ref, panel, own_sem.at[0])
     own_panel.start()
 
-    def columns(det):
-        return beam_ref.at[:, :, :, pl.ds(pl.multiple_of(det * span, span), span)]
-
-    own_beams = pltpu.make_async_copy(columns(me), beams.at[me], own_sem.at[1])
+    def columns(det, orders):
+        return beam_ref.at[:, orders, :, pl.ds(pl.multiple_of(det * span, span), span)]
+
+    every_order = pl.ds(0, MPRIME)
+    own_beams = pltpu.make_async_copy(columns(me, every_order), beams.at[me], own_sem.at[1])
     own_beams.start()
     for load in loads:
         load.wait()
-    for group, row in enumerate(choose_cycles(codes_ref[...], cycles_ref[...])):
-        chosen_ref[group : group + 1, :] = row
+    chosen = choose_cycles(codes_ref[...], cycles_ref[...])
+    for place, hot in enumerate(payload_masks(chosen)):
+        hot_ref[:, place * 128 : place * 128 + 128] = hot
     keys, places = own_blocks(codes_ref[...], owner)
     keys_ref[...] = jnp.broadcast_to(keys, keys_ref.shape)
     pl.semaphore_wait(barrier, bands - 1 + dets - 1)
@@ -289,18 +321,25 @@
             device_id_type=MESH,
         )
 
-    sends = [
-        remote(0, step, columns(peers[step]), beams.at[me]) for step in range(1, dets)
-    ]
-    for copy in sends:
+    cuts = [
+        pl.ds(first, last - first) for first, last in zip(ORDER_CUTS[:-1], ORDER_CUTS[1:])
+    ]
+    beam_sends = [
+        [
+            remote(
+                stage, step, columns(peers[step], orders), beams.at[me, :, orders]
+            )
+            for step in range(1, dets)
+        ]
+        for stage, orders in enumerate(cuts)
+    ]
+    for copy in [copy for stage in beam_sends for copy in stage]:
         copy.start()
     turns = places * orders_ref[...]
     cos_ref[...] = cosine_of_turns(turns).astype(jnp.bfloat16)
     sin_ref[...] = cosine_of_turns(turns + NPHI // 4).astype(jnp.bfloat16)
     own_panel.wait()
     own_beams.wait()
-    for copy in sends:
-        copy.wait()
     real_row = iota((rows, span), 0) % 2 == 0
     direct, crossed = [], []
     for comp in range(comps):
@@ -323,11 +362,18 @@
             part[det, order] = sums[2 * det : 2 * det + 2]
         return carry
 
-    lax.fori_loop(0, MPRIME, one_order, 0)
-    sends = [remote(1, step, part.at[peers[step]], parts.at[me]) for step in range(1, dets)]
-    for copy in sends:
-        copy.start()
-    for copy in sends:
+    sums_sends = []
+    for stage, orders in enumerate(cuts):
+        for copy in beam_sends[stage]:
+            copy.wait()
+        lax.fori_loop(ORDER_CUTS[stage], ORDER_CUTS[stage + 1], one_order, 0)
+        for step in range(1, dets):
+            copy = remote(
+                len(cuts) + stage, step, part.at[peers[step], orders], parts.at[me, orders]
+            )
+            copy.start()
+            sums_sends.append(copy)
+    for copy in sums_sends:
         copy.wait()
     coeff[...] = jnp.zeros_like(coeff)
     for order in range(MPRIME):
@@ -335,13 +381,12 @@
         for step in range(1, dets):
             total = total + parts[peers[step], order]
         coeff[2 * order : 2 * order + 2, :] = total
-    chosen = [chosen_ref[group : group + 1, :] for group in range(4)]
-    payload[...] = gather_payload(coeff[...], psi_ref, chosen).reshape(payload.shape)
+    picked = dot(hot_ref[...], payload_waves(coeff[...], psi_ref))
+    payload[...] = picked.astype(jnp.bfloat16).reshape(payload.shape)
     own = pltpu.make_async_copy(payload.at[owner], received.at[owner], own_sem.at[2])
     own.start()
 
-    def send(step, carry):
-        peer = lax.rem(owner + step, bands)
+    def send(peer):
         pltpu.make_async_remote_copy(
             src_ref=payload.at[peer],
             dst_ref=received.at[owner],
@@ -350,9 +395,21 @@
             device_id={"band": peer},
             device_id_type=MESH,
         ).start()
-        return carry
-
-    lax.fori_loop(1, bands, send, 0)
+
+    far_first(send)
+    keys = keys_ref[:, 0:1]
+    pieces = [
+        slice(first, first + CHUNK) for first in range(0, block_ref.shape[1], CHUNK)
+    ]
+    for piece in pieces:
+        low, high = blend_masks(keys, block_ref[:, piece], cell_ref[:, piece])
+        low_ref[:, piece] = low
+        high_ref[:, piece] = high
+        low_part, high_part = blend_weights(
+            phi_ref[:, piece], frac_ref[0, :, piece], frac_ref[1, :, piece]
+        )
+        low_weight[:, piece] = low_part
+        high_weight[:, piece] = high_part
     own.wait()
     others = pl.ds(0, bands - 1)
     everything = pltpu.make_async_remote_copy(
@@ -367,18 +424,10 @@
     cells = block_cells(
         received[...].reshape(BANDS * ROWS, 128), cos_ref, sin_ref, scale
     )
-    keys = keys_ref[:, 0:1]
-    for first in range(0, block_ref.shape[1], CHUNK):
-        piece = slice(first, first + CHUNK)
-        out_ref[:, piece] = blend(
-            cells,
-            keys,
-            block_ref[:, piece],
-            phi_ref[:, piece],
-            cell_ref[:, piece],
-            frac_ref[0, :, piece],
-            frac_ref[1, :, piece],
-        )
+    for piece in pieces:
+        value = low_weight[:, piece] * dot(cells, low_ref[:, piece])
+        value = value + high_weight[:, piece] * dot(cells, high_ref[:, piece])
+        out_ref[:, piece] = jnp.sum(value, 0, keepdims=True)
     everything.wait_send()
 
 
@@ -424,7 +473,11 @@
             pltpu.VMEM((dets, MPRIME, 2, cycles), jnp.float32),
             pltpu.VMEM((dets, MPRIME, 2, cycles), jnp.float32),
             pltpu.VMEM((ORDERS_PAD, cycles), jnp.float32),
-            pltpu.VMEM((4, BANDS * ROWS), jnp.float32),
+            pltpu.VMEM((BANDS * ROWS, 8 * cycles), jnp.bfloat16),
+            pltpu.VMEM((LISTED * NPSI, samples), jnp.bfloat16),
+            pltpu.VMEM((LISTED * NPSI, samples), jnp.bfloat16),
+            pltpu.VMEM((BLOCK_PHI, samples), jnp.float32),
+            pltpu.VMEM((BLOCK_PHI, samples), jnp.float32),
             pltpu.VMEM((LISTED * NPSI, 128), jnp.int32),
             pltpu.VMEM((LISTED * BLOCK_PHI, orders_all), jnp.bfloat16),
             pltpu.VMEM((LISTED * BLOCK_PHI, orders_all), jnp.bfloat16),
@@ -435,8 +488,8 @@
         + [
             pltpu.SemaphoreType.DMA((len(small),)),
             pltpu.SemaphoreType.DMA((3,)),
-            pltpu.SemaphoreType.DMA((2, dets)),
-            pltpu.SemaphoreType.DMA((2, dets)),
+            pltpu.SemaphoreType.DMA((2 * len(ORDER_CUTS) - 2, dets)),
+            pltpu.SemaphoreType.DMA((2 * len(ORDER_CUTS) - 2, dets)),
             pltpu.SemaphoreType.DMA,
             pltpu.SemaphoreType.DMA,
         ],

time: 44.3 us -> 41.2 us (0.930)
  Pallas kernels: 42.8 us -> 39.7 us
    pallas_call x1, Pallas kernels: 42.8 us -> 39.7 us  [per_device(): pl.pallas_call(functools.partial(signal_kernel, BANDS, dets, scale), out_...]
where the time goes in v4:
time: 41.2 us; the launch traced here: 41 us
  Pallas kernels  39.7 us (96%)
  local copies, waits for them, and re-layouts  1.32 us (3%)
    pallas_call x1, Pallas kernels, per_device(): pl.pallas_call(functools.partial(signal_kernel, BANDS, dets, scale), out_...  39.7 us
    unnamed x1, local copies, waits for them, and re-layouts  1.32 us

profile of v4, /device:TPU:1, one launch (start us, length us, event | category | flops | bytes accessed | tf_op | source)
XLA Modules:
  0.0 41.0 jit_solution(5883054281882028382)
XLA Ops:
  0.0 39.7 %shard_map.109 = f32[1,4096]{1,0:T(1,128)} custom-call(bf16[3,17,2,2048]{3,2,1,0:T(2,128)(2,1)} %bitcast.13, bf16[17,512,128]{2,1,0:T(8,128)(2,1)} %bitcast.12, f32[6,1,512]{2,1,0:T(1,128)} %bitcast.15, f32[2,40,128]{2,1,0:T(8,128)} %constant.2.clone.psi_in, s32[256,128]{1,0:T(8,128)} %bitcast.14, s32[3,128]{1,0:T(4,128)} %bitcast.16, s32[1,128]{1,0:T(1,128)} %bitcast.17, ...), custom_call_target="tpu_custom_call" | custom-call | tf_op jit(solution)/shard_map/pallas_call | solution.py:465
  39.7 1.3 %copy.13 = f32[1,4096]{1,0:T(1,128)} copy(f32[1,4096]{1,0:T(1,128)} %shard_map.109) | data formatting | bytes 32768

commit v5 on v4

--- a/solution.py
+++ b/solution.py
@@ -20,7 +20,7 @@
 ORDERS_PAD = 40
 CHUNK = 512
 LINE = 16
-ORDER_CUTS = (0, 6, 12, 17)
+ORDER_CUTS = (0, 5, 10, 14, 17)
 UNLISTED = 200.0
 MESH = pl.DeviceIdType.MESH
 
@@ -296,11 +296,17 @@
     own_panel = pltpu.make_async_copy(panel_ref, panel, own_sem.at[0])
     own_panel.start()
 
+    shared = span // 2
+    core = lax.rem(owner, 2)
+    partner = owner + 1 - 2 * core
+    share = pl.ds(pl.multiple_of(core * shared, shared), shared)
+
     def columns(det, orders):
-        return beam_ref.at[:, orders, :, pl.ds(pl.multiple_of(det * span, span), span)]
-
-    every_order = pl.ds(0, MPRIME)
-    own_beams = pltpu.make_async_copy(columns(me, every_order), beams.at[me], own_sem.at[1])
+        first = pl.multiple_of(det * span + core * shared, shared)
+        return beam_ref.at[:, orders, :, pl.ds(first, shared)]
+
+    own_columns = beam_ref.at[:, :, :, pl.ds(pl.multiple_of(me * span, span), span)]
+    own_beams = pltpu.make_async_copy(own_columns, beams.at[me], own_sem.at[1])
     own_beams.start()
     for load in loads:
         load.wait()
@@ -327,7 +333,7 @@
     beam_sends = [
         [
             remote(
-                stage, step, columns(peers[step], orders), beams.at[me, :, orders]
+                stage, step, columns(peers[step], orders), beams.at[me, :, orders, :, share]
             )
             for step in range(1, dets)
         ]
@@ -362,10 +368,30 @@
             part[det, order] = sums[2 * det : 2 * det + 2]
         return carry
 
+    def hand_over(stage):
+        copies = []
+        for step in range(1, dets):
+            beam_sends[stage][step - 1].wait()
+            place = beams.at[peers[dets - step], :, cuts[stage], :, share]
+            copy = pltpu.make_async_remote_copy(
+                src_ref=place,
+                dst_ref=place,
+                send_sem=send_sem.at[2 * len(cuts) + stage, step],
+                recv_sem=recv_sem.at[2 * len(cuts) + stage, step],
+                device_id={"band": partner},
+                device_id_type=MESH,
+            )
+            copy.start()
+            copies.append(copy)
+        return copies
+
     sums_sends = []
+    handed = hand_over(0)
     for stage, orders in enumerate(cuts):
-        for copy in beam_sends[stage]:
+        ahead = hand_over(stage + 1) if stage + 1 < len(cuts) else []
+        for copy in handed:
             copy.wait()
+        handed = ahead
         lax.fori_loop(ORDER_CUTS[stage], ORDER_CUTS[stage + 1], one_order, 0)
         for step in range(1, dets):
             copy = remote(
@@ -488,8 +514,8 @@
         + [
             pltpu.SemaphoreType.DMA((len(small),)),
             pltpu.SemaphoreType.DMA((3,)),
-            pltpu.SemaphoreType.DMA((2 * len(ORDER_CUTS) - 2, dets)),
-            pltpu.SemaphoreType.DMA((2 * len(ORDER_CUTS) - 2, dets)),
+            pltpu.SemaphoreType.DMA((3 * len(ORDER_CUTS) - 3, dets)),
+            pltpu.SemaphoreType.DMA((3 * len(ORDER_CUTS) - 3, dets)),
             pltpu.SemaphoreType.DMA,
             pltpu.SemaphoreType.DMA,
         ],

time: 41.2 us -> 41.8 us (1.015)
  Pallas kernels: 39.7 us -> 40.3 us
    pallas_call x1, Pallas kernels: 39.7 us -> 40.3 us  [per_device(): pl.pallas_call(functools.partial(signal_kernel, BANDS, dets, scale), out_...]
where the time goes in v5:
time: 41.8 us; the launch traced here: 41.6 us
  Pallas kernels  40.3 us (96%)
  local copies, waits for them, and re-layouts  1.32 us (3%)
    pallas_call x1, Pallas kernels, per_device(): pl.pallas_call(functools.partial(signal_kernel, BANDS, dets, scale), out_...  40.3 us
    unnamed x1, local copies, waits for them, and re-layouts  1.32 us

profile of v5, /device:TPU:1, one launch (start us, length us, event | category | flops | bytes accessed | tf_op | source)
XLA Modules:
  0.0 41.6 jit_solution(5839958170279948688)
XLA Ops:
  0.0 40.3 %shard_map.109 = f32[1,4096]{1,0:T(1,128)} custom-call(bf16[3,17,2,2048]{3,2,1,0:T(2,128)(2,1)} %bitcast.13, bf16[17,512,128]{2,1,0:T(8,128)(2,1)} %bitcast.12, f32[6,1,512]{2,1,0:T(1,128)} %bitcast.15, f32[2,40,128]{2,1,0:T(8,128)} %constant.2.clone.psi_in, s32[256,128]{1,0:T(8,128)} %bitcast.14, s32[3,128]{1,0:T(4,128)} %bitcast.16, s32[1,128]{1,0:T(1,128)} %bitcast.17, ...), custom_call_target="tpu_custom_call" | custom-call | tf_op jit(solution)/shard_map/pallas_call | solution.py:491
  40.3 1.3 %copy.13 = f32[1,4096]{1,0:T(1,128)} copy(f32[1,4096]{1,0:T(1,128)} %shard_map.109) | data formatting | bytes 32768

commit v6 on v4

--- a/solution.py
+++ b/solution.py
@@ -366,7 +366,7 @@
     for stage, orders in enumerate(cuts):
         for copy in beam_sends[stage]:
             copy.wait()
-        lax.fori_loop(ORDER_CUTS[stage], ORDER_CUTS[stage + 1], one_order, 0)
+        lax.fori_loop(ORDER_CUTS[stage], ORDER_CUTS[stage + 1], one_order, 0, unroll=True)
         for step in range(1, dets):
             copy = remote(
                 len(cuts) + stage, step, part.at[peers[step], orders], parts.at[me, orders]

time: 41.2 us -> 40.7 us (0.988)
  Pallas kernels: 39.7 us -> 39.2 us
    pallas_call x1, Pallas kernels: 39.7 us -> 39.2 us  [per_device(): pl.pallas_call(functools.partial(signal_kernel, BANDS, dets, scale), out_...]
where the time goes in v6:
time: 40.7 us; the launch traced here: 40.5 us
  Pallas kernels  39.2 us (96%)
  local copies, waits for them, and re-layouts  1.32 us (3%)
    pallas_call x1, Pallas kernels, per_device(): pl.pallas_call(functools.partial(signal_kernel, BANDS, dets, scale), out_...  39.2 us
    unnamed x1, local copies, waits for them, and re-layouts  1.32 us

profile of v6, /device:TPU:1, one launch (start us, length us, event | category | flops | bytes accessed | tf_op | source)
XLA Modules:
  0.0 40.5 jit_solution(4542176830527609326)
XLA Ops:
  0.0 39.2 %shard_map.109 = f32[1,4096]{1,0:T(1,128)} custom-call(bf16[3,17,2,2048]{3,2,1,0:T(2,128)(2,1)} %bitcast.13, bf16[17,512,128]{2,1,0:T(8,128)(2,1)} %bitcast.12, f32[6,1,512]{2,1,0:T(1,128)} %bitcast.15, f32[2,40,128]{2,1,0:T(8,128)} %constant.2.clone.psi_in, s32[256,128]{1,0:T(8,128)} %bitcast.14, s32[3,128]{1,0:T(4,128)} %bitcast.16, s32[1,128]{1,0:T(1,128)} %bitcast.17, ...), custom_call_target="tpu_custom_call" | custom-call | tf_op jit(solution)/shard_map/pallas_call | solution.py:465
  39.2 1.3 %copy.13 = f32[1,4096]{1,0:T(1,128)} copy(f32[1,4096]{1,0:T(1,128)} %shard_map.109) | data formatting | bytes 32768
